TPU v7x, 768 devices: a whole 4x8x12 slice. The times are simulated.
768 devices in a mesh: rows: 64 (over y, z_hi, core), rep: 12 (over z_lo, x).
Axes of the slice: x: 4, y: 8, z: 12 (z_hi: 4, z_lo: 3; z = z_hi * 3 + z_lo), core: 2. Of those that a mesh axis runs over, the one named last changes fastest.
Arguments:
- features: bfloat16 [98304, 256], P(('rows', 'rep')), may hold values from -6 to 6
- weight: bfloat16 [256, 256], replicated, may hold values from -0.375 to 0.375
- tiles: bfloat16 [64, 12, 12, 8, 128, 128], P('rows', 'rep'), as said below
- send_src: int32 [64, 12, 64, 24], P('rows', 'rep'), may hold values from 0 to 12287, as said below
- send_dst: int32 [64, 12, 64, 24], P('rows', 'rep'), may hold values from 0 to 128, as said below
- cotangent: bfloat16 [98304, 256], P(('rows', 'rep')), may hold values from -6 to 6
Outputs:
- output: bfloat16 [98304, 256], P(('rows', 'rep'))
- grad_w: float32 [256, 256], replicated
- grad_x: bfloat16 [98304, 256], P(('rows', 'rep'))
Inputs may be any that keep to these rules, and one draw needn't show every extreme that they name: Device (g, c)'s tiles are nonnegative; a tile row is nonzero only if some live slot of that device names it. `send_src`: A flattened tile row (b * 8 + k) * 128 + i of the sending device. Each tile row is named by at most one live slot, and all live slots naming rows of one tile belong to one peer p. An empty slot holds 0. `send_dst`: 128 marks an empty slot. For each rep index c there is a peer p to which every device (g, c) sends all 24 slots live, and some device has an empty slot. Destination rows may repeat.
All inputs are finite; a program needn't handle non-finite values.
Results may differ from a plain program's by a relative error of at most 0.02.
Values may be sent and summed in bfloat16 or wider, within the bound.
A program may use at most 64 MiB of HBM per device.

v0:
```python
import math

import jax
import jax.numpy as jnp
from jax import lax
from jax.sharding import PartitionSpec as P


def local(features, weight, tiles, send_src, send_dst, cotangent):
    blocks = tiles[0, 0]
    source = send_src[0, 0]
    target = send_dst[0, 0]
    rows_dev = features.shape[0]
    feature_width = features.shape[1]
    col_blocks = blocks.shape[0]
    per_col = blocks.shape[1]
    block_size = blocks.shape[2]
    tile_rows = col_blocks * per_col * block_size
    whole_group = lax.all_gather(features, "rep", axis=0, tiled=True)
    partial_value = jnp.einsum(
        "bkij,bjf->bkif",
        blocks,
        whole_group.reshape(col_blocks, block_size, feature_width),
        preferred_element_type=jnp.float32,
    )
    flattened = partial_value.reshape(tile_rows, feature_width)
    outgoing = flattened[source]
    incoming, landing = (
        lax.all_to_all(outgoing, "rows", split_axis=0, concat_axis=0, tiled=True),
        lax.all_to_all(target, "rows", split_axis=0, concat_axis=0, tiled=True),
    )
    summed = (
        features.astype(jnp.float32)
        .at[landing.reshape(-1)]
        .add(incoming.reshape(-1, feature_width), mode="drop")
    )
    aggregated = summed.astype(jnp.bfloat16)
    preact = jnp.dot(aggregated, weight, preferred_element_type=jnp.float32)
    sigmoid = jax.nn.sigmoid(preact)
    output = (preact * sigmoid).astype(jnp.bfloat16)
    pre_grad = (cotangent.astype(jnp.float32) * sigmoid * (1.0 + preact * (1.0 - sigmoid))).astype(
        jnp.bfloat16
    )
    local_w = jnp.einsum("nf,ng->fg", aggregated, pre_grad, preferred_element_type=jnp.float32)
    node_count = rows_dev * lax.axis_size("rows") * lax.axis_size("rep")
    grad_w = lax.psum(local_w, ("rows", "rep")) * (1.0 / math.sqrt(node_count))
    back_in = jnp.einsum("ng,fg->nf", pre_grad, weight, preferred_element_type=jnp.float32).astype(
        jnp.bfloat16
    )
    requested = back_in[jnp.minimum(landing, rows_dev - 1)]
    returned = lax.all_to_all(requested, "rows", split_axis=0, concat_axis=0, tiled=True)
    placed = jnp.where(target < rows_dev, source, tile_rows)
    spread = (
        jnp.zeros((tile_rows, feature_width), jnp.bfloat16)
        .at[placed.reshape(-1)]
        .set(returned.reshape(-1, feature_width), mode="drop")
    )
    spread = spread.reshape(col_blocks, per_col, block_size, feature_width)
    group_rows = col_blocks * block_size
    group_terms = jnp.einsum(
        "bkij,bkif->bjf", blocks, spread, preferred_element_type=jnp.float32
    ).reshape(group_rows, feature_width)
    group_total = lax.psum(group_terms.astype(jnp.bfloat16), "rep").astype(jnp.float32)
    transposed = lax.dynamic_slice_in_dim(
        group_total, lax.axis_index("rep") * rows_dev, rows_dev, 0
    )
    grad_x = (back_in.astype(jnp.float32) + transposed).astype(jnp.bfloat16)
    return (output, grad_w, grad_x)


def solution(mesh):
    placed = (
        P(("rows", "rep"), None),
        P(),
        P("rows", "rep", None, None, None, None),
        P("rows", "rep", None, None),
        P("rows", "rep", None, None),
        P(("rows", "rep"), None),
    )
    return jax.shard_map(
        local,
        mesh=mesh,
        in_specs=placed,
        out_specs=(P(("rows", "rep"), None), P(), P(("rows", "rep"), None)),
        check_vma=False,
    )
```

profile of v0, /device:TPU:1, one launch (start us, length us, event | category | flops | bytes accessed | tf_op | source)
XLA Modules:
  0.0 808.0 jit_solution(16647759001466855441)
XLA Ops:
  7.2 1.6 copy.15
  8.7 21.8 %all-to-all-start = ((s32[64,1,24]{2,1,0:T(1,128)}), s32[64,1,24]{2,1,0:T(1,128)S(1)}, u32[]{:S(2)}, u32[]{:S(2)}) async-start(s32[64,1,24]{2,1,0:T(1,128)} %bitcast), calls=%async_computation | async-start | bytes 65536 | tf_op jit(solution)/shard_map/all_to_all | solution.py:30
  30.6 30.1 %all_gather.3 = bf16[1536,256]{1,0:T(8,128)(2,1)} all-gather(bf16[128,256]{1,0:T(8,128)(2,1)} %param.6), channel_id=1, replica_groups=mesh['rows'=64,'rep'=12] {'rep'}, dimensions={0}, use_global_device_ids=true | all-gather | bytes 851968 | tf_op jit(solution)/shard_map/all_gather | solution.py:19
  60.7 0.8 copy.16
  61.6 7.5 fusion.2
  69.0 9.2 %gather_fusion = f32[1536,256]{1,0:T(8,128)} fusion(f32[12288,256]{1,0:T(8,128)} %bitcast.38, s32[2048]{0:T(1024)S(1)} %pad_clamp_fusion.1), kind=kCustom, calls=%fused_computation | custom fusion | bytes 3151872 | tf_op jit(solution)/shard_map/gather | solution.py:27
  78.3 26.0 %all-to-all-start.1 = ((f32[64,24,256]{2,1,0:T(8,128)}), f32[64,24,256]{2,1,0:T(8,128)}, u32[]{:S(2)}, u32[]{:S(2)}) async-start(f32[64,24,256]{2,1,0:T(8,128)} %bitcast.41), calls=%async_computation.1 | async-start | bytes 3145728 | tf_op jit(solution)/shard_map/all_to_all | solution.py:29
  104.3 0.5 broadcast.123
  104.8 0.7 broadcast_minimum_fusion
  105.8 61.6 %all-to-all-done.1 = f32[64,24,256]{2,1,0:T(8,128)} async-done(((f32[64,24,256]{2,1,0:T(8,128)}), f32[64,24,256]{2,1,0:T(8,128)}, u32[]{:S(2)}, u32[]{:S(2)}) %all-to-all-start.1) | async-done | bytes 1572896 | tf_op jit(solution)/shard_map/all_to_all | solution.py:29
  167.4 9.4 %scatter_fusion = f32[128,256]{1,0:T(8,128)S(1)} fusion(f32[128,256]{1,0:T(8,128)S(1)} %convert_element_type.36, s32[1536]{0:T(1024)S(1)} %fusion.12, f32[1536,256]{1,0:T(8,128)} %bitcast.8), kind=kCustom, calls=%fused_computation.2 | custom fusion | flops 393216 | bytes 4724736 | tf_op jit(solution)/shard_map/scatter-add | solution.py:35
  176.8 0.8 multiply_convert_fusion.1
  177.6 0.6 copy-done.6
  178.5 5.4 gather_fusion.1
  183.9 17.2 %all-to-all-start.2 = ((bf16[64,24,256]{2,1,0:T(8,128)(2,1)}), bf16[64,24,256]{2,1,0:T(8,128)(2,1)}, u32[]{:S(2)}, u32[]{:S(2)}) async-start(bf16[64,24,256]{2,1,0:T(8,128)(2,1)} %bitcast.43), calls=%async_computation.2 | async-start | bytes 1572864 | tf_op jit(solution)/shard_map/all_to_all | solution.py:51
  201.3 1.8 fusion.8
  203.2 0.2 all-reduce.5.cloned.1.call-start
  203.4 29.6 %all-to-all-done.2 = bf16[64,24,256]{2,1,0:T(8,128)(2,1)} async-done(((bf16[64,24,256]{2,1,0:T(8,128)(2,1)}), bf16[64,24,256]{2,1,0:T(8,128)(2,1)}, u32[]{:S(2)}, u32[]{:S(2)}) %all-to-all-start.2) | async-done | bytes 786464 | tf_op jit(solution)/shard_map/all_to_all | solution.py:51
  233.0 11.4 %scatter_custom_fusion.1 = bf16[12288,256]{1,0:T(8,128)(2,1)} fusion(s32[1536]{0:T(1024)S(1)} %fusion.13, bf16[1536,256]{1,0:T(8,128)(2,1)} %bitcast.11, bf16[]{:T(256)} %constant.14.clone.1), kind=kCustom, calls=%fused_computation.8 | custom fusion | bytes 6291968 | tf_op jit(solution)/shard_map/scatter | solution.py:56
  244.4 4.9 bitcast_convert_fusion
  249.4 421.2 %all-reduce.3.cloned.1.call-done = f32[256,256]{1,0:T(8,128)} async-done(((f32[256,256]{1,0:T(8,128)}), f32[256,256]{1,0:T(8,128)}) %all-reduce.3.cloned.1.call-update) | async-done | bytes 262160 | tf_op jit(solution)/shard_map/psum | solution.py:46
  670.6 1.7 broadcast_multiply_fusion
  672.3 127.4 %all-reduce.5.cloned.1.call-done = bf16[1536,256]{1,0:T(8,128)(2,1)} async-done(((bf16[1536,256]{1,0:T(8,128)(2,1)}), bf16[1536,256]{1,0:T(8,128)(2,1)}) %all-reduce.5.cloned.1.call-update) | async-done | bytes 786448 | tf_op jit(solution)/shard_map/psum | solution.py:63
  799.7 1.5 add_convert_fusion
  (31 shorter events, 0.8 us)
Async XLA Ops:
  7.2 54.4 %copy-start = (bf16[1,1,12,8,128,128]{5,4,3,2,1,0:T(8,128)(2,1)S(1)}, bf16[1,1,12,8,128,128]{5,4,3,2,1,0:T(8,128)(2,1)}, u32[]{:S(2)}) copy-start(bf16[1,1,12,8,128,128]{5,4,3,2,1,0:T(8,128)(2,1)} %param.8) | copy-start | bytes 9437188
  8.7 69.5 %all-to-all-start = ((s32[64,1,24]{2,1,0:T(1,128)}), s32[64,1,24]{2,1,0:T(1,128)S(1)}, u32[]{:S(2)}, u32[]{:S(2)}) async-start(s32[64,1,24]{2,1,0:T(1,128)} %bitcast), calls=%async_computation | async-start | bytes 65536 | tf_op jit(solution)/shard_map/all_to_all | solution.py:30
  78.3 26.0 %copy-start.1 = (bf16[128,256]{1,0:T(8,128)(2,1)S(1)}, bf16[128,256]{1,0:T(8,128)(2,1)}, u32[]{:S(2)}) copy-start(bf16[128,256]{1,0:T(8,128)(2,1)} %param.6) | copy-start | bytes 196612
  78.3 89.2 %all-to-all-start.1 = ((f32[64,24,256]{2,1,0:T(8,128)}), f32[64,24,256]{2,1,0:T(8,128)}, u32[]{:S(2)}, u32[]{:S(2)}) async-start(f32[64,24,256]{2,1,0:T(8,128)} %bitcast.41), calls=%async_computation.1 | async-start | bytes 3145728 | tf_op jit(solution)/shard_map/all_to_all | solution.py:29
  167.4 9.4 %copy-start.4 = (bf16[256,256]{1,0:T(8,128)(2,1)S(1)}, bf16[256,256]{1,0:T(8,128)(2,1)}, u32[]{:S(2)}) copy-start(bf16[256,256]{1,0:T(8,128)(2,1)} %param.7) | copy-start | bytes 393220
  167.4 10.9 %copy-start.5 = (bf16[128,256]{1,0:T(8,128)(2,1)S(1)}, bf16[128,256]{1,0:T(8,128)(2,1)}, u32[]{:S(2)}) copy-start(bf16[128,256]{1,0:T(8,128)(2,1)} %param.11) | copy-start | bytes 196612
  177.6 0.7 copy-start.6
  178.5 22.6 %copy-start.2 = (s32[1,1,64,24]{2,3,1,0:T(8,128)S(1)}, s32[1,1,64,24]{2,3,1,0:T(8,128)}, u32[]{:S(2)}) copy-start(s32[1,1,64,24]{2,3,1,0:T(8,128)} %param.10) | copy-start | bytes 18436
  178.5 22.6 %copy-start.3 = (s32[1,1,64,24]{2,3,1,0:T(8,128)S(1)}, s32[1,1,64,24]{2,3,1,0:T(8,128)}, u32[]{:S(2)}) copy-start(s32[1,1,64,24]{2,3,1,0:T(8,128)} %param.9) | copy-start | bytes 18436
  183.9 49.2 %all-to-all-start.2 = ((bf16[64,24,256]{2,1,0:T(8,128)(2,1)}), bf16[64,24,256]{2,1,0:T(8,128)(2,1)}, u32[]{:S(2)}, u32[]{:S(2)}) async-start(bf16[64,24,256]{2,1,0:T(8,128)(2,1)} %bitcast.43), calls=%async_computation.2 | async-start | bytes 1572864 | tf_op jit(solution)/shard_map/all_to_all | solution.py:51
  201.1 469.5 %all-reduce.3.cloned.1.call-start = ((), (), s32[]{:S(2)}) async-start(), calls=%async_computation.3 | async-start | bytes 524288 | tf_op jit(solution)/shard_map/psum | solution.py:46
  203.2 596.4 %all-reduce.5.cloned.1.call-start = ((), (), s32[]{:S(2)}) async-start(), calls=%async_computation.4 | async-start | bytes 1572864 | tf_op jit(solution)/shard_map/psum | solution.py:63
Sparse Core Ops, SparseCore 0:
  207.9 462.6 all-reduce.2
  674.1 125.4 all-reduce.4
where the time goes:
time: 819 us; the launch traced here: 808 us
  waiting for transfers between devices  640 us (78%)
  starting transfers between devices  65.2 us (8%)
  blocking collectives  30.1 us (4%)
  local copies, waits for them, and re-layouts  29.9 us (4%)
  matrix products  15.2 us (2%)
  between operations  14.2 us (2%)
  other arithmetic  13.4 us (2%)
    psum x1, waiting for transfers between devices, local(): grad_w = lax.psum(local_w, ('rows', 'rep')) * (1.0 / math.sqrt(node_count))  421 us
    psum x1, waiting for transfers between devices, local(): lax.psum(group_terms.astype(jnp.bfloat16), 'rep').astype(jnp.float32)  127 us
    all_to_all x1, waiting for transfers between devices, local(): lax.all_to_all(outgoing, 'rows', split_axis=0, concat_axis=0, tiled=True)  61.6 us
    all_gather x1, blocking collectives, local(): whole_group = lax.all_gather(features, 'rep', axis=0, tiled=True)  30.1 us
    all_to_all x1, waiting for transfers between devices, local(): lax.all_to_all(requested, 'rows', split_axis=0, concat_axis=0, tiled=True)  29.6 us
    all_to_all x1, starting transfers between devices, local(): lax.all_to_all(outgoing, 'rows', split_axis=0, concat_axis=0, tiled=True)  26 us
    all_to_all x1, starting transfers between devices, local(): lax.all_to_all(target, 'rows', split_axis=0, concat_axis=0, tiled=True)  21.8 us
    all_to_all x1, starting transfers between devices, local(): lax.all_to_all(requested, 'rows', split_axis=0, concat_axis=0, tiled=True)  17.2 us
  transfers between devices with their start and end apart: 5, of which 4 were waited for; matrix products, arithmetic and copies ran while one was open for 5% of the time, Pallas kernels for 0%

commit v1 on v0

v1 whole, which is shorter than its diff:
```python
import math

import jax
import jax.numpy as jnp
from jax import lax
from jax.experimental import pallas as pl
from jax.experimental.pallas import tpu as pltpu
from jax.sharding import PartitionSpec as P

MESH = pl.DeviceIdType.MESH
BF = jnp.bfloat16
F32 = jnp.float32

NY, ZH, NC, ZL, NX = 8, 4, 2, 3, 4
NJ = NY * NC
NREP = ZL * NX
NM = NC * NX
NZ = ZH * ZL
SLOT = 24
MSG = ZH * SLOT
BLK = 128
F = 256
PER_COL = 8
NCOL = 12
NODES = 98304


def _copy(src, dst, ssem, rsem, rows, rep):
    return pltpu.make_async_remote_copy(
        src_ref=src,
        dst_ref=dst,
        send_sem=ssem,
        recv_sem=rsem,
        device_id=(rows, rep),
        device_id_type=MESH,
    )


def _kernel(
    feat, weight, cot, tiles, src, bid, key,
    out, gw, gx,
    X, tb, tf, G, A, AT, keys, U, s1, r1, acc, s2, r2, BI, s3, R, ts, town, rs,
    W, WA, w1, WB, WC, WD, WE,
    loc_sem, ag_s, ag_r, k_s, k_r, y1_s, y1_r, z1_s, z1_r, z2_s, z2_r, y2_s, y2_r,
    rs_s, rs_r, a_s, a_r, b_s, b_r, c_s, c_r, d_s, d_r, e_s, e_r,
):
    r = lax.axis_index("rows")
    c = lax.axis_index("rep")
    y, zh, core = r // (ZH * NC), (r // NC) % ZH, r % NC
    zl, x = c // NX, c % NX
    j = y * NC + core
    m = core * NX + x
    z = zh * ZL + zl

    def row_of(yy, hh, cc):
        return (yy * ZH + hh) * NC + cc

    def plane(jj):
        return row_of(jj // NC, zh, jj % NC), c

    def column(hh):
        return row_of(y, hh, core), c

    def pair(mm):
        return row_of(y, zh, mm // NX), zl * NX + mm % NX

    def along_y(yy):
        return row_of(yy, zh, core), c

    def along_z(zz):
        return row_of(y, zz // ZL, core), (zz % ZL) * NX + x

    def each(count, me, fn):
        def step(k, carry):
            fn((me + k) % count)
            return carry

        lax.fori_loop(1, count, step, 0)

    def ag(cc, own):
        return _copy(feat, X.at[own], ag_s.at[cc], ag_r.at[own], r, cc)

    def kx(jj, own):
        return _copy(key.at[jj], keys.at[own], k_s.at[jj], k_r.at[own], *plane(jj))

    def y1(jj, own):
        return _copy(s1.at[jj], r1.at[own, pl.ds(0, MSG)], y1_s.at[jj], y1_r.at[own], *plane(jj))

    def z1(hh, own):
        return _copy(s2.at[hh], r2.at[own], z1_s.at[hh], z1_r.at[own], *column(hh))

    def z2(hh, own):
        return _copy(BI.at[zh], BI.at[own], z2_s.at[hh], z2_r.at[own], *column(hh))

    def y2(jj, own):
        return _copy(s3.at[jj], R.at[own, pl.ds(0, MSG)], y2_s.at[jj], y2_r.at[own], *plane(jj))

    def rx(cc, own):
        return _copy(ts.at[cc], rs.at[own], rs_s.at[cc], rs_r.at[own], r, cc)

    def ga(mm, own):
        return _copy(W.at[mm], WA.at[own], a_s.at[mm], a_r.at[own], *pair(mm))

    def gb(yy, own):
        return _copy(w1.at[yy], WB.at[own], b_s.at[yy], b_r.at[own], *along_y(yy))

    def gc(zz, own):
        return _copy(WC.at[z], WC.at[own], c_s.at[zz], c_r.at[own], *along_z(zz))

    def gd(yy, own):
        return _copy(WD.at[y], WD.at[own], d_s.at[yy], d_r.at[own], *along_y(yy))

    def ge(mm, own):
        return _copy(WE.at[m], WE.at[own], e_s.at[mm], e_r.at[own], *pair(mm))

    def start(make, count, me):
        each(count, me, lambda o: make(o, me).start())

    def arrive(make, count, me):
        each(count, me, lambda o: make(o, o).wait_recv())

    def sent(make, count, me):
        each(count, me, lambda o: make(o, me).wait_send())

    load = pltpu.make_async_copy(tiles, tb, loc_sem)
    load.start()

    barrier = pltpu.get_barrier_semaphore()

    def greet(rows, rep):
        pl.semaphore_signal(barrier, inc=1, device_id=(rows, rep), device_id_type=MESH)

    each(NREP, c, lambda cc: greet(r, cc))
    each(NJ, j, lambda jj: greet(*plane(jj)))
    each(ZH, zh, lambda hh: greet(*column(hh)))
    each(NX, x, lambda xx: greet(row_of(y, zh, 1 - core), zl * NX + xx))
    each(ZH, zh, lambda hh: each(ZL, zl, lambda ll: greet(row_of(y, hh, core), ll * NX + x)))
    pl.semaphore_wait(barrier, (NREP - 1) + (NJ - 1) + (ZH - 1) + (NX - 1) + (ZH - 1) * (ZL - 1))

    start(ag, NREP, c)
    start(kx, NJ, j)
    X[c] = feat[...]
    keys[j] = key[j]

    def clear(jj, carry):
        r1[jj, MSG:BLK, :] = jnp.zeros((BLK - MSG, F), BF)
        R[jj, MSG:BLK, :] = jnp.zeros((BLK - MSG, F), BF)
        return carry

    lax.fori_loop(0, NJ, clear, 0)

    load.wait()

    def widen(t, carry):
        at = pl.multiple_of(t * BLK, BLK)
        tf[pl.ds(at, BLK), :] = tb[pl.ds(at, BLK), :].astype(F32)
        return carry

    lax.fori_loop(0, NCOL * PER_COL, widen, 0)

    def column_of(row):
        return jnp.transpose(jnp.broadcast_to(row, (BLK, BLK)))

    def gather(jj, carry):
        for i in range(MSG):
            G[jj, i : i + 1, :] = tf[pl.ds(src[jj, i], 1), :]
        rows = G[jj, 0:MSG, :]
        where = column_of(bid[jj].astype(F32))[0:MSG, :]
        for b in range(NCOL):
            A[jj, :, b * BLK : (b + 1) * BLK] = jnp.where(where == b, rows, 0.0).astype(BF)
        return carry

    lax.fori_loop(0, NJ, gather, 0)

    arrive(ag, NREP, c)

    for t in range(NJ // 4):
        at = ((j // 4 + t) % 4) * 4
        rows = jnp.dot(
            A[pl.ds(at, 4)].reshape(4 * MSG, NCOL * BLK),
            X[...].reshape(NREP * BLK, F),
            preferred_element_type=F32,
        )
        s1[pl.ds(at, 4)] = rows.reshape(4, MSG, F).astype(BF)
        for u in range(4):
            jj = at + (j + u) % 4

            @pl.when(jj != j)
            def _():
                y1(jj, j).start()

    r1[j, 0:MSG, :] = s1[j]

    arrive(kx, NJ, j)
    lanes = lax.broadcasted_iota(jnp.int32, (MSG, BLK), 1).astype(F32)

    def mirror(jj, carry):
        where = column_of(keys[jj].astype(F32))[0:MSG, :]
        for h in range(ZH):
            U[jj, :, h * BLK : (h + 1) * BLK] = jnp.where(
                where == lanes + float(h * BLK), 1.0, 0.0
            ).astype(BF)
        turned = jnp.transpose(G[jj])
        row = bid[jj].astype(F32)
        at = pl.multiple_of(jj * BLK, BLK)
        for b in range(NCOL):
            AT[b, :, pl.ds(at, BLK)] = jnp.where(row == b, turned, 0.0).astype(BF)
        return carry

    lax.fori_loop(0, NJ, mirror, 0)

    heads = lax.broadcasted_iota(jnp.int32, (ZH * BLK, BLK), 0)

    def picked(jj):
        hot = jnp.where(keys[jj] == heads, 1.0, 0.0).astype(BF)
        return jnp.dot(hot, r1[jj], preferred_element_type=F32).reshape(ZH, BLK, F)

    acc[...] = picked(j)

    def add_rows(k, carry):
        jj = (j + k) % NJ
        y1(jj, jj).wait_recv()
        acc[...] += picked(jj)
        return carry

    lax.fori_loop(1, NJ, add_rows, 0)

    for k in range(1, ZH):
        hh = (zh + k) % ZH
        s2[hh] = acc[hh].astype(BF)
        z1(hh, zh).start()
    summed = feat[...].astype(F32) + acc[zh]
    arrive(z1, ZH, zh)
    for k in range(1, ZH):
        summed += r2[(zh + k) % ZH].astype(F32)
    aggregated = summed.astype(BF)

    preact = jnp.dot(aggregated, weight[...], preferred_element_type=F32)
    sigmoid = jax.nn.sigmoid(preact)
    pre_grad = (cot[...].astype(F32) * sigmoid * (1.0 + preact * (1.0 - sigmoid))).astype(BF)
    back_in = lax.dot_general(
        pre_grad, weight[...], (((1,), (1,)), ((), ())), preferred_element_type=F32
    ).astype(BF)
    BI[zh] = back_in
    start(z2, ZH, zh)

    out[...] = (preact * sigmoid).astype(BF)
    local_w = lax.dot_general(
        aggregated, pre_grad, (((0,), (0,)), ((), ())), preferred_element_type=F32
    )
    W[0 : NM // 2] = local_w[:, 0:BLK].reshape(NM // 2, NY, 8, BLK)
    W[NM // 2 : NM] = local_w[:, BLK:F].reshape(NM // 2, NY, 8, BLK)
    start(ga, NM, m)

    arrive(z2, ZH, zh)
    for t in range(NJ // 4):
        at = ((j // 4 + t) % 4) * 4
        rows = jnp.dot(
            U[pl.ds(at, 4)].reshape(4 * MSG, ZH * BLK),
            BI[...].reshape(ZH * BLK, F),
            preferred_element_type=F32,
        )
        s3[pl.ds(at, 4)] = rows.reshape(4, MSG, F).astype(BF)
        for u in range(4):
            jj = at + (j + u) % 4

            @pl.when(jj != j)
            def _():
                y2(jj, j).start()

    R[j, 0:MSG, :] = s3[j]

    arrive(ga, NM, m)
    total = W[m]
    for k in range(1, NM):
        total += WA[(m + k) % NM]
    w1[...] = total
    start(gb, NY, y)
    arrive(gb, NY, y)
    total = w1[y]
    for k in range(1, NY):
        total += WB[(y + k) % NY]
    WC[z] = total
    start(gc, NZ, z)
    arrive(gc, NZ, z)
    total = WC[0]
    for k in range(1, NZ):
        total += WC[k]
    WD[y] = total * (1.0 / math.sqrt(NODES))
    start(gd, NY, y)
    arrive(gd, NY, y)
    WE[m] = WD[...]
    start(ge, NM, m)

    arrive(y2, NJ, j)
    for t in range(ZL):
        at = ((zl + t) % ZL) * NX
        terms = jnp.dot(
            AT[pl.ds(at, NX)].reshape(NX * BLK, NJ * BLK),
            R[...].reshape(NJ * BLK, F),
            preferred_element_type=F32,
        ).reshape(NX, BLK, F)
        ts[pl.ds(at, NX)] = terms.astype(BF)
        if t == 0:
            town[...] = terms
        for u in range(NX):
            cc = at + (x + u) % NX

            @pl.when(cc != c)
            def _():
                rx(cc, c).start()

    arrive(ge, NM, m)
    for half in range(2):
        gw[:, half * BLK : (half + 1) * BLK] = WE[half * NM // 2 : (half + 1) * NM // 2].reshape(
            F, BLK
        )

    result = BI[zh].astype(F32) + town[x]
    arrive(rx, NREP, c)
    for k in range(1, NREP):
        result += rs[(c + k) % NREP].astype(F32)
    gx[...] = result.astype(BF)

    for make, count, me in (
        (ag, NREP, c), (kx, NJ, j), (y1, NJ, j), (z1, ZH, zh), (z2, ZH, zh), (y2, NJ, j),
        (rx, NREP, c), (ga, NM, m), (gb, NY, y), (gc, NZ, z), (gd, NY, y), (ge, NM, m),
    ):
        sent(make, count, me)


def local(features, weight, tiles, send_src, send_dst, cotangent):
    def ordered(a):
        return a.reshape(NY, ZH, NC, SLOT).transpose(0, 2, 1, 3).reshape(NJ, MSG)

    source = ordered(send_src[0, 0])
    target = ordered(send_dst[0, 0])
    step = jnp.repeat(jnp.arange(ZH, dtype=jnp.int32) * BLK, SLOT)[None, :]
    pad = ((0, 0), (0, BLK - MSG))
    key = jnp.where(target < BLK, target + step, -1)
    key = jnp.pad(key, pad, constant_values=-1).reshape(NJ, 1, BLK)
    bid = jnp.pad(source // (PER_COL * BLK), pad, constant_values=-1).reshape(NJ, 1, BLK)
    V = pltpu.VMEM
    dma = pltpu.SemaphoreType.DMA
    vmem = pl.BlockSpec(memory_space=pltpu.VMEM)
    rows = NCOL * PER_COL * BLK
    return pl.pallas_call(
        _kernel,
        out_shape=(
            jax.ShapeDtypeStruct((BLK, F), BF),
            jax.ShapeDtypeStruct((F, F), F32),
            jax.ShapeDtypeStruct((BLK, F), BF),
        ),
        in_specs=[
            vmem, vmem, vmem, pl.BlockSpec(memory_space=pl.ANY),
            pl.BlockSpec(memory_space=pltpu.SMEM), vmem, vmem,
        ],
        out_specs=(vmem, vmem, vmem),
        scratch_shapes=[
            V((NREP, BLK, F), BF),
            V((rows, BLK), BF),
            V((rows, BLK), F32),
            V((NJ, BLK, BLK), F32),
            V((NJ, MSG, NCOL * BLK), BF),
            V((NCOL, BLK, NJ * BLK), BF),
            V((NJ, 1, BLK), jnp.int32),
            V((NJ, MSG, ZH * BLK), BF),
            V((NJ, MSG, F), BF),
            V((NJ, BLK, F), BF),
            V((ZH, BLK, F), F32),
            V((ZH, BLK, F), BF),
            V((ZH, BLK, F), BF),
            V((ZH, BLK, F), BF),
            V((NJ, MSG, F), BF),
            V((NJ, BLK, F), BF),
            V((NREP, BLK, F), BF),
            V((NX, BLK, F), F32),
            V((NREP, BLK, F), BF),
            V((NM, NY, 8, BLK), F32),
            V((NM, NY, 8, BLK), F32),
            V((NY, 8, BLK), F32),
            V((NY, 8, BLK), F32),
            V((NZ, 8, BLK), F32),
            V((NY, 8, BLK), F32),
            V((NM, NY, 8, BLK), F32),
            dma,
            *[dma((n,)) for n in (NREP, NJ, NJ, ZH, ZH, NJ, NREP, NM, NY, NZ, NY, NM) for _ in range(2)],
        ],
        compiler_params=pltpu.CompilerParams(
            collective_id=0, has_side_effects=True, vmem_limit_bytes=56 * 1024 * 1024
        ),
    )(features, weight, cotangent, tiles.reshape(rows, BLK), source, bid, key)


def solution(mesh):
    placed = (
        P(("rows", "rep"), None),
        P(),
        P("rows", "rep", None, None, None, None),
        P("rows", "rep", None, None),
        P("rows", "rep", None, None),
        P(("rows", "rep"), None),
    )
    return jax.shard_map(
        local,
        mesh=mesh,
        in_specs=placed,
        out_specs=(P(("rows", "rep"), None), P(), P(("rows", "rep"), None)),
        check_vma=False,
    )
```

time: 819 us -> 140 us (0.17); the launches traced: 808 us -> 139 us
  waiting for transfers between devices: 640 us -> 0 us
  Pallas kernels: 0 us -> 130 us
  starting transfers between devices: 65.2 us -> 0 us
  blocking collectives: 30.1 us -> 0 us
  local copies, waits for them, and re-layouts: 29.9 us -> 7.74 us
  matrix products: 15.2 us -> 0 us
  between operations: 14.2 us -> 0.67 us
  other arithmetic: 13.4 us -> 0.02 us
    psum x2 -> x0, waiting for transfers between devices: 549 us -> none  [the longest x1 421 us: local(): grad_w = lax.psum(local_w, ('rows', 'rep')) * (1.0 / math.sqrt(node_count))]
    pallas_call x0 -> x1, Pallas kernels: none -> 130 us  [local(): pl.pallas_call(_kernel, out_shape=(jax.ShapeDtypeStruct((BLK, F), BF), ja...]
    all_to_all x3 -> x0, waiting for transfers between devices: 91.2 us -> none  [the longest x1 61.6 us: local(): lax.all_to_all(outgoing, 'rows', split_axis=0, concat_axis=0, tiled=True)]
    all_to_all x3 -> x0, starting transfers between devices: 65 us -> none  [the longest x1 26 us: local(): lax.all_to_all(outgoing, 'rows', split_axis=0, concat_axis=0, tiled=True)]
    all_gather x1 -> x0, blocking collectives: 30.1 us -> none  [local(): whole_group = lax.all_gather(features, 'rep', axis=0, tiled=True)]
    dot_general x5 -> x0, matrix products: 15.2 us -> none  [the longest x1 7.47 us: local(): jnp.einsum('bkij,bjf->bkif', blocks, whole_group.reshape(col_blocks, bloc...]
    gather x2 -> x0, local copies, waits for them, and re-layouts: 14.6 us -> none  [the longest x1 9.22 us: local(): outgoing = flattened[source]]
    scatter x1 -> x0, local copies, waits for them, and re-layouts: 11.4 us -> none  [local(): spread = jnp.zeros((tile_rows, feature_width), jnp.bfloat16).at[placed.re...]
  transfers between devices with their start and end apart: 5 -> 0, of which waited for: 4 -> 0; matrix products, arithmetic and copies ran while one was open for 5% -> 0% of each run, Pallas kernels for 0% -> 0%
where the time goes in v1:
time: 140 us; the launch traced here: 139 us
  Pallas kernels  130 us (93%)
  local copies, waits for them, and re-layouts  7.74 us (6%)
    pallas_call x1, Pallas kernels, local(): pl.pallas_call(_kernel, out_shape=(jax.ShapeDtypeStruct((BLK, F), BF), ja...  130 us
    unnamed x7, local copies, waits for them, and re-layouts  6.19 us

profile of v1, /device:TPU:1, one launch (start us, length us, event | category | flops | bytes accessed | tf_op | source)
XLA Modules:
  0.0 138.7 jit_solution(10439658892638958638)
XLA Ops:
  0.6 0.1 broadcast_in_dim.5
  0.7 0.1 add.15
  0.8 0.8 copy.12
  1.6 0.1 reshape.23.src
  1.7 0.0 copy-start
  1.7 0.6 pad.7
  2.3 0.8 copy.14
  3.1 0.1 reshape.25
  3.2 0.6 pad.8
  3.8 0.0 copy-done
  3.8 130.3 %shard_map.85 = (bf16[128,256]{1,0:T(8,128)(2,1)}, f32[256,256]{1,0:T(8,128)}, bf16[128,256]{1,0:T(8,128)(2,1)}) custom-call(bf16[128,256]{1,0:T(8,128)(2,1)} %feat.1, bf16[256,256]{1,0:T(8,128)(2,1)} %weight.1, bf16[128,256]{1,0:T(8,128)(2,1)} %cot.1, bf16[12288,128]{1,0:T(8,128)(2,1)} %bitcast.11, s32[16,96]{1,0:T(8,128)} %copy-done, ...), custom_call_target="tpu_custom_call" | custom-call | tf_op jit(solution)/shard_map/pallas_call | solution.py:347
  134.1 1.5 %copy.20 = bf16[128,256]{1,0:T(8,128)(2,1)} copy(bf16[128,256]{1,0:T(8,128)(2,1)} %get-tuple-element.6) | data formatting | bytes 131072
  135.6 1.7 %copy.21 = f32[256,256]{1,0:T(8,128)} copy(f32[256,256]{1,0:T(8,128)} %get-tuple-element.7) | data formatting | bytes 524288
  137.3 1.5 %copy.22 = bf16[128,256]{1,0:T(8,128)(2,1)} copy(bf16[128,256]{1,0:T(8,128)(2,1)} %get-tuple-element.8) | data formatting | bytes 131072
  (5 shorter events, 0.0 us)
Async XLA Ops:
  1.7 2.1 %copy-start = (s32[16,96]{1,0:T(8,128)}, s32[16,96]{1,0:T(8,128)S(1)}, u32[]{:S(2)}) copy-start(s32[16,96]{1,0:T(8,128)S(1)} %reshape.23.src) | copy-start | bytes 18436

commit v2 on v1

v2 whole, which is shorter than its diff:
```python
import math

import jax
import jax.numpy as jnp
from jax import lax
from jax.experimental import pallas as pl
from jax.experimental.pallas import tpu as pltpu
from jax.sharding import PartitionSpec as P

MESH = pl.DeviceIdType.MESH
BF = jnp.bfloat16
F32 = jnp.float32

NY, ZH, NC, ZL, NX = 8, 4, 2, 3, 4
NJ = NY * NC
NREP = ZL * NX
NM = NC * NX
NZ = ZH * ZL
SLOT = 24
MSG = ZH * SLOT
BLK = 128
F = 256
PER_COL = 8
NCOL = 12
NODES = 98304


def _copy(src, dst, ssem, rsem, rows, rep):
    return pltpu.make_async_remote_copy(
        src_ref=src,
        dst_ref=dst,
        send_sem=ssem,
        recv_sem=rsem,
        device_id=(rows, rep),
        device_id_type=MESH,
    )


def _kernel(
    feat, weight, cot, tiles, src, meta,
    out, gw, gx,
    X, tb, tf, G, A, AT, keys, U, T, s1, r1, acc, s2, r2, BI, s3, R, ts, town, rs,
    W, WA, w1, WB, WC, WD, WE,
    loc_sem, ag_s, ag_r, k_s, k_r, y1_s, y1_r, z1_s, z1_r, z2_s, z2_r, y2_s, y2_r,
    rs_s, rs_r, a_s, a_r, b_s, b_r, c_s, c_r, d_s, d_r, e_s, e_r,
):
    r = lax.axis_index("rows")
    c = lax.axis_index("rep")
    y, zh, core = lax.div(r, ZH * NC), lax.rem(lax.div(r, NC), ZH), lax.rem(r, NC)
    zl, x = lax.div(c, NX), lax.rem(c, NX)
    j = y * NC + core
    m = core * NX + x
    z = zh * ZL + zl

    def row_of(yy, hh, cc):
        return (yy * ZH + hh) * NC + cc

    def plane(jj):
        return row_of(lax.div(jj, NC), zh, lax.rem(jj, NC)), c

    def column(hh):
        return row_of(y, hh, core), c

    def pair(mm):
        return row_of(y, zh, lax.div(mm, NX)), zl * NX + lax.rem(mm, NX)

    def along_y(yy):
        return row_of(yy, zh, core), c

    def along_z(zz):
        return row_of(y, lax.div(zz, ZL), core), lax.rem(zz, ZL) * NX + x

    def each(count, me, fn):
        def step(k, carry):
            fn(lax.rem(me + k, count))
            return carry

        lax.fori_loop(1, count, step, 0)

    def ag(h):
        return lambda o, own: _copy(X.at[h, c], X.at[h, own], ag_s.at[h, o], ag_r.at[h, own], r, o)

    def y1(h):
        return lambda o, own: _copy(
            s1.at[h, o], r1.at[h, own, pl.ds(0, MSG)], y1_s.at[h, o], y1_r.at[h, own], *plane(o)
        )

    def z1(h):
        return lambda o, own: _copy(
            s2.at[h, o], r2.at[h, own], z1_s.at[h, o], z1_r.at[h, own], *column(o)
        )

    def z2(h):
        return lambda o, own: _copy(
            BI.at[h, zh], BI.at[h, own], z2_s.at[h, o], z2_r.at[h, own], *column(o)
        )

    def y2(h):
        return lambda o, own: _copy(
            s3.at[h, o], R.at[h, own, pl.ds(0, MSG)], y2_s.at[h, o], y2_r.at[h, own], *plane(o)
        )

    def rx(h):
        return lambda o, own: _copy(
            ts.at[h, o], rs.at[h, own], rs_s.at[h, o], rs_r.at[h, own], r, o
        )

    def kx(o, own):
        return _copy(meta.at[NJ + o], keys.at[own], k_s.at[o], k_r.at[own], *plane(o))

    def ga(o, own):
        return _copy(W.at[o], WA.at[own], a_s.at[o], a_r.at[own], *pair(o))

    def gb(o, own):
        return _copy(w1.at[o], WB.at[own], b_s.at[o], b_r.at[own], *along_y(o))

    def gc(o, own):
        return _copy(WC.at[z], WC.at[own], c_s.at[o], c_r.at[own], *along_z(o))

    def gd(o, own):
        return _copy(WD.at[y], WD.at[own], d_s.at[o], d_r.at[own], *along_y(o))

    def ge(o, own):
        return _copy(WE.at[m], WE.at[own], e_s.at[o], e_r.at[own], *pair(o))

    def start(make, count, me):
        each(count, me, lambda o: make(o, me).start())

    def arrive(make, count, me):
        each(count, me, lambda o: make(o, o).wait_recv())

    def sent(make, count, me):
        each(count, me, lambda o: make(o, me).wait_send())

    load = pltpu.make_async_copy(tiles, tb, loc_sem)
    load.start()

    barrier = pltpu.get_barrier_semaphore()

    def greet(rows, rep):
        pl.semaphore_signal(barrier, inc=1, device_id=(rows, rep), device_id_type=MESH)

    each(NREP, c, lambda cc: greet(r, cc))
    each(NJ, j, lambda jj: greet(*plane(jj)))
    each(ZH, zh, lambda hh: greet(*column(hh)))
    each(NX, x, lambda xx: greet(row_of(y, zh, 1 - core), zl * NX + xx))
    each(ZH, zh, lambda hh: each(ZL, zl, lambda ll: greet(row_of(y, hh, core), ll * NX + x)))
    for h in range(2):
        X[h, c] = feat[:, h * BLK : (h + 1) * BLK]
    pl.semaphore_wait(barrier, (NREP - 1) + (NJ - 1) + (ZH - 1) + (NX - 1) + (ZH - 1) * (ZL - 1))

    for h in range(2):
        start(ag(h), NREP, c)
    start(kx, NJ, j)
    keys[j] = meta[NJ + j]

    def clear(jj, carry):
        for h in range(2):
            r1[h, jj, MSG:BLK, :] = jnp.zeros((BLK - MSG, BLK), BF)
            R[h, jj, MSG:BLK, :] = jnp.zeros((BLK - MSG, BLK), BF)
        return carry

    lax.fori_loop(0, NJ, clear, 0)

    load.wait()

    def widen(t, carry):
        at = pl.multiple_of(t * BLK, BLK)
        tf[pl.ds(at, BLK), :] = tb[pl.ds(at, BLK), :].astype(F32)
        return carry

    lax.fori_loop(0, NCOL * PER_COL, widen, 0)

    def block_of(jj):
        return lax.shift_right_arithmetic(meta[jj], 10).astype(F32)

    def column_of(row):
        return jnp.transpose(jnp.broadcast_to(row, (BLK, BLK)))

    def gather(jj, carry):
        for i in range(MSG):
            G[jj, i : i + 1, :] = tf[pl.ds(src[jj, i], 1), :]
        rows = G[jj, 0:MSG, :]
        where = column_of(block_of(jj))[0:MSG, :]
        for b in range(NCOL):
            A[jj, :, b * BLK : (b + 1) * BLK] = jnp.where(where == b, rows, 0.0).astype(BF)
        return carry

    lax.fori_loop(0, NJ, gather, 0)

    def fan_out(h, left, right, width, held, make):
        for t in range(NJ // 4):
            at = lax.rem(lax.div(j, 4) + t, 4) * 4
            rows = jnp.dot(
                left[pl.ds(at, 4)].reshape(4 * MSG, width), right, preferred_element_type=F32
            )
            held[h, pl.ds(at, 4)] = rows.reshape(4, MSG, BLK).astype(BF)
            for u in range(4):
                o = at + lax.rem(j + u, 4)

                @pl.when(o != j)
                def _():
                    make(o, j).start()

    for h in range(2):
        arrive(ag(h), NREP, c)
        fan_out(h, A, X[h].reshape(NREP * BLK, BLK), NREP * BLK, s1, y1(h))
        r1[h, j, 0:MSG, :] = s1[h, j]

    arrive(kx, NJ, j)
    lanes = lax.broadcasted_iota(jnp.int32, (MSG, BLK), 1).astype(F32)
    heads = lax.broadcasted_iota(jnp.int32, (ZH * BLK, BLK), 0)

    def mirror(jj, carry):
        at = pl.multiple_of(jj * BLK, BLK)
        T[:, pl.ds(at, BLK)] = jnp.where(keys[jj] == heads, 1.0, 0.0).astype(BF)
        where = column_of(keys[jj].astype(F32))[0:MSG, :]
        for h in range(ZH):
            U[jj, :, h * BLK : (h + 1) * BLK] = jnp.where(
                where == lanes + float(h * BLK), 1.0, 0.0
            ).astype(BF)
        turned = jnp.transpose(G[jj])
        row = block_of(jj)
        for b in range(NCOL):
            AT[b, :, pl.ds(at, BLK)] = jnp.where(row == b, turned, 0.0).astype(BF)
        return carry

    lax.fori_loop(0, NJ, mirror, 0)

    for h in range(2):
        arrive(y1(h), NJ, j)
        acc[h] = jnp.dot(
            T[...], r1[h].reshape(NJ * BLK, BLK), preferred_element_type=F32
        ).reshape(ZH, BLK, BLK)
        for k in range(1, ZH):
            o = lax.rem(zh + k, ZH)
            s2[h, o] = acc[h, o].astype(BF)
            z1(h)(o, zh).start()

    halves = []
    for h in range(2):
        total = feat[:, h * BLK : (h + 1) * BLK].astype(F32) + acc[h, zh]
        arrive(z1(h), ZH, zh)
        for k in range(1, ZH):
            total += r2[h, lax.rem(zh + k, ZH)].astype(F32)
        halves.append(total.astype(BF))
    aggregated = jnp.concatenate(halves, axis=1)

    preact = jnp.dot(aggregated, weight[...], preferred_element_type=F32)
    sigmoid = jax.nn.sigmoid(preact)
    pre_grad = (cot[...].astype(F32) * sigmoid * (1.0 + preact * (1.0 - sigmoid))).astype(BF)
    back_in = lax.dot_general(
        pre_grad, weight[...], (((1,), (1,)), ((), ())), preferred_element_type=F32
    ).astype(BF)
    for h in range(2):
        BI[h, zh] = back_in[:, h * BLK : (h + 1) * BLK]
        start(z2(h), ZH, zh)

    local_w = lax.dot_general(
        aggregated, pre_grad, (((0,), (0,)), ((), ())), preferred_element_type=F32
    )
    W[0 : NM // 2] = local_w[:, 0:BLK].reshape(NM // 2, NY, 8, BLK)
    W[NM // 2 : NM] = local_w[:, BLK:F].reshape(NM // 2, NY, 8, BLK)
    start(ga, NM, m)
    out[...] = (preact * sigmoid).astype(BF)
    arrive(ga, NM, m)
    total = W[m]
    for k in range(1, NM):
        total += WA[lax.rem(m + k, NM)]
    w1[...] = total
    start(gb, NY, y)

    for h in range(2):
        arrive(z2(h), ZH, zh)
        fan_out(h, U, BI[h].reshape(ZH * BLK, BLK), ZH * BLK, s3, y2(h))
        R[h, j, 0:MSG, :] = s3[h, j]

    arrive(gb, NY, y)
    total = w1[y]
    for k in range(1, NY):
        total += WB[lax.rem(y + k, NY)]
    WC[z] = total
    start(gc, NZ, z)
    arrive(gc, NZ, z)
    total = WC[0]
    for k in range(1, NZ):
        total += WC[k]
    WD[y] = total * (1.0 / math.sqrt(NODES))
    start(gd, NY, y)

    for h in range(2):
        arrive(y2(h), NJ, j)
        for t in range(ZL):
            at = lax.rem(zl + t, ZL) * NX
            terms = jnp.dot(
                AT[pl.ds(at, NX)].reshape(NX * BLK, NJ * BLK),
                R[h].reshape(NJ * BLK, BLK),
                preferred_element_type=F32,
            ).reshape(NX, BLK, BLK)
            ts[h, pl.ds(at, NX)] = terms.astype(BF)
            if t == 0:
                town[h] = terms
            for u in range(NX):
                o = at + lax.rem(x + u, NX)

                @pl.when(o != c)
                def _():
                    rx(h)(o, c).start()

        if h == 0:
            arrive(gd, NY, y)
            WE[m] = WD[...]
            start(ge, NM, m)

    for h in range(2):
        result = BI[h, zh].astype(F32) + town[h, x]
        arrive(rx(h), NREP, c)
        for k in range(1, NREP):
            result += rs[h, lax.rem(c + k, NREP)].astype(F32)
        gx[:, h * BLK : (h + 1) * BLK] = result.astype(BF)

    arrive(ge, NM, m)
    for h in range(2):
        gw[:, h * BLK : (h + 1) * BLK] = WE[h * NM // 2 : (h + 1) * NM // 2].reshape(F, BLK)

    for make, count, me in (
        (ag, NREP, c), (y1, NJ, j), (z1, ZH, zh), (z2, ZH, zh), (y2, NJ, j), (rx, NREP, c),
    ):
        for h in range(2):
            sent(make(h), count, me)
    for make, count, me in (
        (kx, NJ, j), (ga, NM, m), (gb, NY, y), (gc, NZ, z), (gd, NY, y), (ge, NM, m),
    ):
        sent(make, count, me)


def _leave(a, b, c, aa, bb, cc, sems):
    copies = [
        pltpu.make_async_copy(s, d, sems.at[i]) for i, (s, d) in enumerate(((a, aa), (b, bb), (c, cc)))
    ]
    for copy in copies:
        copy.start()
    for copy in copies:
        copy.wait()


def local(features, weight, tiles, send_src, send_dst, cotangent):
    head = jnp.arange(ZH, dtype=jnp.int32)[None, :, None, None] * BLK
    target = send_dst[0, 0].reshape(NY, ZH, NC, SLOT)
    key = jnp.where(target < BLK, target + head, -1)
    both = jnp.stack([send_src[0, 0].reshape(NY, ZH, NC, SLOT), key])
    both = both.transpose(0, 1, 3, 2, 4).reshape(2 * NJ, MSG)
    both = jnp.pad(both, ((0, 0), (0, BLK - MSG)), constant_values=-1)
    V = pltpu.VMEM
    dma = pltpu.SemaphoreType.DMA
    vmem = pl.BlockSpec(memory_space=pltpu.VMEM)
    hbm = pl.BlockSpec(memory_space=pl.ANY)
    rows = NCOL * PER_COL * BLK
    shapes = (
        jax.ShapeDtypeStruct((BLK, F), BF),
        jax.ShapeDtypeStruct((F, F), F32),
        jax.ShapeDtypeStruct((BLK, F), BF),
    )
    outs = pl.pallas_call(
        _kernel,
        out_shape=shapes,
        in_specs=[vmem, vmem, vmem, hbm, pl.BlockSpec(memory_space=pltpu.SMEM), vmem],
        out_specs=(vmem, vmem, vmem),
        scratch_shapes=[
            V((2, NREP, BLK, BLK), BF),
            V((rows, BLK), BF),
            V((rows, BLK), F32),
            V((NJ, BLK, BLK), F32),
            V((NJ, MSG, NCOL * BLK), BF),
            V((NCOL, BLK, NJ * BLK), BF),
            V((NJ, 1, BLK), jnp.int32),
            V((NJ, MSG, ZH * BLK), BF),
            V((ZH * BLK, NJ * BLK), BF),
            V((2, NJ, MSG, BLK), BF),
            V((2, NJ, BLK, BLK), BF),
            V((2, ZH, BLK, BLK), F32),
            V((2, ZH, BLK, BLK), BF),
            V((2, ZH, BLK, BLK), BF),
            V((2, ZH, BLK, BLK), BF),
            V((2, NJ, MSG, BLK), BF),
            V((2, NJ, BLK, BLK), BF),
            V((2, NREP, BLK, BLK), BF),
            V((2, NX, BLK, BLK), F32),
            V((2, NREP, BLK, BLK), BF),
            V((NM, NY, 8, BLK), F32),
            V((NM, NY, 8, BLK), F32),
            V((NY, 8, BLK), F32),
            V((NY, 8, BLK), F32),
            V((NZ, 8, BLK), F32),
            V((NY, 8, BLK), F32),
            V((NM, NY, 8, BLK), F32),
            dma,
            dma((2, NREP)), dma((2, NREP)), dma((NJ,)), dma((NJ,)), dma((2, NJ)), dma((2, NJ)),
            dma((2, ZH)), dma((2, ZH)), dma((2, ZH)), dma((2, ZH)), dma((2, NJ)), dma((2, NJ)),
            dma((2, NREP)), dma((2, NREP)),
            *[dma((n,)) for n in (NM, NY, NZ, NY, NM) for _ in range(2)],
        ],
        compiler_params=pltpu.CompilerParams(
            collective_id=0, has_side_effects=True, vmem_limit_bytes=56 * 1024 * 1024
        ),
    )(features, weight, cotangent, tiles.reshape(rows, BLK), both, both.reshape(2 * NJ, 1, BLK))
    return pl.pallas_call(
        _leave,
        out_shape=shapes,
        in_specs=[hbm] * 3,
        out_specs=(hbm,) * 3,
        scratch_shapes=[dma((3,))],
    )(*outs)


def solution(mesh):
    placed = (
        P(("rows", "rep"), None),
        P(),
        P("rows", "rep", None, None, None, None),
        P("rows", "rep", None, None),
        P("rows", "rep", None, None),
        P(("rows", "rep"), None),
    )
    return jax.shard_map(
        local,
        mesh=mesh,
        in_specs=placed,
        out_specs=(P(("rows", "rep"), None), P(), P(("rows", "rep"), None)),
        check_vma=False,
    )
```

time: 140 us -> 122 us (0.87)
  Pallas kernels: 130 us -> 119 us
  local copies, waits for them, and re-layouts: 7.74 us -> 2.31 us
    pallas_call x1 -> x2, Pallas kernels: 130 us -> 119 us  [the longest x1 106 us: local(): pl.pallas_call(_kernel, out_shape=shapes, in_specs=[vmem, vmem, vmem, hbm...]
    unnamed x7 -> x2, local copies, waits for them, and re-layouts: 6.19 us -> 1.58 us
where the time goes in v2:
time: 122 us
  Pallas kernels  119 us (98%)
  local copies, waits for them, and re-layouts  2.31 us (2%)
    pallas_call x1, Pallas kernels, local(): pl.pallas_call(_kernel, out_shape=shapes, in_specs=[vmem, vmem, vmem, hbm...  106 us
    pallas_call x1, Pallas kernels, local(): pl.pallas_call(_leave, out_shape=shapes, in_specs=[hbm] * 3, out_specs=(h...  13 us

profile of v2, /device:TPU:1, one launch (start us, length us, event | category | flops | bytes accessed | tf_op | source)
XLA Modules:
  0.0 121.9 jit_solution(12405894626901917)
XLA Ops:
  0.6 0.8 copy.12
  1.4 0.8 copy.13
  2.2 0.1 compare_select_fusion
  2.4 0.1 reshape.43
  2.5 0.6 pad.4.src
  3.1 105.8 %shard_map.85 = (bf16[128,256]{1,0:T(8,128)(2,1)}, f32[256,256]{1,0:T(8,128)}, bf16[128,256]{1,0:T(8,128)(2,1)}) custom-call(bf16[128,256]{1,0:T(8,128)(2,1)} %feat.1, bf16[256,256]{1,0:T(8,128)(2,1)} %weight.1, bf16[128,256]{1,0:T(8,128)(2,1)} %cot.1, bf16[12288,128]{1,0:T(8,128)(2,1)} %bitcast.6, s32[32,128]{1,0:T(8,128)} %pad.4.src, s32[32,1,128]{2,1,0:T(1,128)} %bitcast.7), custom_call_target="tpu_custom_call" | custom-call | tf_op jit(solution)/shard_map/pallas_call | solution.py:364
  108.9 13.0 %shard_map.86 = (bf16[128,256]{1,0:T(8,128)(2,1)}, f32[256,256]{1,0:T(8,128)}, bf16[128,256]{1,0:T(8,128)(2,1)}) custom-call(bf16[128,256]{1,0:T(8,128)(2,1)} %get-tuple-element.6.a, f32[256,256]{1,0:T(8,128)} %get-tuple-element.7.b, bf16[128,256]{1,0:T(8,128)(2,1)} %get-tuple-element.8.c), custom_call_target="tpu_custom_call" | custom-call | tf_op jit(solution)/shard_map/pallas_call | solution.py:407
  (3 shorter events, 0.1 us)

commit v3 on v2

--- a/solution.py
+++ b/solution.py
@@ -37,9 +37,9 @@
 
 
 def _kernel(
-    feat, weight, cot, tiles, src, meta,
+    feat, weight, cot, tiles, src, srcs, dsts,
     out, gw, gx,
-    X, tb, tf, G, A, AT, keys, U, T, s1, r1, acc, s2, r2, BI, s3, R, ts, town, rs,
+    X, tb, tf, G, A, AT, bcol, brow, krow, keys, U, T, s1, r1, acc, s2, r2, BI, s3, R, ts, town, rs,
     W, WA, w1, WB, WC, WD, WE,
     loc_sem, ag_s, ag_r, k_s, k_r, y1_s, y1_r, z1_s, z1_r, z2_s, z2_r, y2_s, y2_r,
     rs_s, rs_r, a_s, a_r, b_s, b_r, c_s, c_r, d_s, d_r, e_s, e_r,
@@ -106,7 +106,7 @@
         )
 
     def kx(o, own):
-        return _copy(meta.at[NJ + o], keys.at[own], k_s.at[o], k_r.at[own], *plane(o))
+        return _copy(krow.at[o], keys.at[own], k_s.at[o], k_r.at[own], *plane(o))
 
     def ga(o, own):
         return _copy(W.at[o], WA.at[own], a_s.at[o], a_r.at[own], *pair(o))
@@ -151,8 +151,6 @@
 
     for h in range(2):
         start(ag(h), NREP, c)
-    start(kx, NJ, j)
-    keys[j] = meta[NJ + j]
 
     def clear(jj, carry):
         for h in range(2):
@@ -171,17 +169,29 @@
 
     lax.fori_loop(0, NCOL * PER_COL, widen, 0)
 
-    def block_of(jj):
-        return lax.shift_right_arithmetic(meta[jj], 10).astype(F32)
-
-    def column_of(row):
-        return jnp.transpose(jnp.broadcast_to(row, (BLK, BLK)))
+    block = lax.shift_right_arithmetic(srcs[...], 10).astype(F32)
+    landing = dsts[...].astype(F32)
+    padding = jnp.full((BLK - MSG, BLK), -1.0, F32)
+    for jj in range(NJ):
+        peers = [((jj // NC) * ZH + h) * NC + jj % NC for h in range(ZH)]
+        blocks = [jnp.broadcast_to(block[:, p : p + 1], (SLOT, BLK)) for p in peers]
+        heads = [jnp.broadcast_to(landing[:, p : p + 1], (SLOT, BLK)) for p in peers]
+        heads = [jnp.where(v < BLK, v + float(h * BLK), -1.0) for h, v in enumerate(heads)]
+        blocks = jnp.concatenate([*blocks, padding], axis=0)
+        bcol[jj] = blocks[0:MSG]
+        brow[jj] = jnp.transpose(blocks)[0:1]
+        krow[jj] = jnp.transpose(jnp.concatenate([*heads, padding], axis=0))[0:1]
+    start(kx, NJ, j)
+    keys[j] = krow[j]
 
     def gather(jj, carry):
-        for i in range(MSG):
-            G[jj, i : i + 1, :] = tf[pl.ds(src[jj, i], 1), :]
+        first = lax.div(jj, NC) * (ZH * NC) + lax.rem(jj, NC)
+        for h in range(ZH):
+            for i in range(SLOT):
+                at = h * SLOT + i
+                G[jj, at : at + 1, :] = tf[pl.ds(src[i, first + h * NC], 1), :]
         rows = G[jj, 0:MSG, :]
-        where = column_of(block_of(jj))[0:MSG, :]
+        where = bcol[jj]
         for b in range(NCOL):
             A[jj, :, b * BLK : (b + 1) * BLK] = jnp.where(where == b, rows, 0.0).astype(BF)
         return carry
@@ -209,18 +219,18 @@
 
     arrive(kx, NJ, j)
     lanes = lax.broadcasted_iota(jnp.int32, (MSG, BLK), 1).astype(F32)
-    heads = lax.broadcasted_iota(jnp.int32, (ZH * BLK, BLK), 0)
+    heads = lax.broadcasted_iota(jnp.int32, (ZH * BLK, BLK), 0).astype(F32)
 
     def mirror(jj, carry):
         at = pl.multiple_of(jj * BLK, BLK)
         T[:, pl.ds(at, BLK)] = jnp.where(keys[jj] == heads, 1.0, 0.0).astype(BF)
-        where = column_of(keys[jj].astype(F32))[0:MSG, :]
+        where = jnp.transpose(jnp.broadcast_to(keys[jj], (BLK, BLK)))[0:MSG, :]
         for h in range(ZH):
             U[jj, :, h * BLK : (h + 1) * BLK] = jnp.where(
                 where == lanes + float(h * BLK), 1.0, 0.0
             ).astype(BF)
         turned = jnp.transpose(G[jj])
-        row = block_of(jj)
+        row = brow[jj]
         for b in range(NCOL):
             AT[b, :, pl.ds(at, BLK)] = jnp.where(row == b, turned, 0.0).astype(BF)
         return carry
@@ -334,23 +344,15 @@
         sent(make, count, me)
 
 
-def _leave(a, b, c, aa, bb, cc, sems):
-    copies = [
-        pltpu.make_async_copy(s, d, sems.at[i]) for i, (s, d) in enumerate(((a, aa), (b, bb), (c, cc)))
-    ]
-    for copy in copies:
-        copy.start()
-    for copy in copies:
-        copy.wait()
+def _leave(a, b, c, aa, bb, cc):
+    aa[...] = a[...]
+    bb[...] = b[...]
+    cc[...] = c[...]
 
 
 def local(features, weight, tiles, send_src, send_dst, cotangent):
-    head = jnp.arange(ZH, dtype=jnp.int32)[None, :, None, None] * BLK
-    target = send_dst[0, 0].reshape(NY, ZH, NC, SLOT)
-    key = jnp.where(target < BLK, target + head, -1)
-    both = jnp.stack([send_src[0, 0].reshape(NY, ZH, NC, SLOT), key])
-    both = both.transpose(0, 1, 3, 2, 4).reshape(2 * NJ, MSG)
-    both = jnp.pad(both, ((0, 0), (0, BLK - MSG)), constant_values=-1)
+    source = send_src[0, 0].T
+    target = send_dst[0, 0].T
     V = pltpu.VMEM
     dma = pltpu.SemaphoreType.DMA
     vmem = pl.BlockSpec(memory_space=pltpu.VMEM)
@@ -364,7 +366,7 @@
     outs = pl.pallas_call(
         _kernel,
         out_shape=shapes,
-        in_specs=[vmem, vmem, vmem, hbm, pl.BlockSpec(memory_space=pltpu.SMEM), vmem],
+        in_specs=[vmem, vmem, vmem, hbm, pl.BlockSpec(memory_space=pltpu.SMEM), vmem, vmem],
         out_specs=(vmem, vmem, vmem),
         scratch_shapes=[
             V((2, NREP, BLK, BLK), BF),
@@ -373,7 +375,10 @@
             V((NJ, BLK, BLK), F32),
             V((NJ, MSG, NCOL * BLK), BF),
             V((NCOL, BLK, NJ * BLK), BF),
-            V((NJ, 1, BLK), jnp.int32),
+            V((NJ, MSG, BLK), F32),
+            V((NJ, 1, BLK), F32),
+            V((NJ, 1, BLK), F32),
+            V((NJ, 1, BLK), F32),
             V((NJ, MSG, ZH * BLK), BF),
             V((ZH * BLK, NJ * BLK), BF),
             V((2, NJ, MSG, BLK), BF),
@@ -403,13 +408,12 @@
         compiler_params=pltpu.CompilerParams(
             collective_id=0, has_side_effects=True, vmem_limit_bytes=56 * 1024 * 1024
         ),
-    )(features, weight, cotangent, tiles.reshape(rows, BLK), both, both.reshape(2 * NJ, 1, BLK))
+    )(features, weight, cotangent, tiles.reshape(rows, BLK), source, source, target)
     return pl.pallas_call(
         _leave,
         out_shape=shapes,
-        in_specs=[hbm] * 3,
-        out_specs=(hbm,) * 3,
-        scratch_shapes=[dma((3,))],
+        in_specs=[vmem] * 3,
+        out_specs=(vmem,) * 3,
     )(*outs)
 
 

time: 122 us -> 107 us (0.88)
  Pallas kernels: 119 us -> 106 us
  local copies, waits for them, and re-layouts: 2.31 us -> 0 us
    pallas_call x1, Pallas kernels: 13 us -> 1.71 us  [local(): pl.pallas_call(_leave, out_shape=shapes, in_specs=[vmem] * 3, out_specs=(...]
    unnamed x2 -> x0, local copies, waits for them, and re-layouts: 1.58 us -> none
    pallas_call x1, Pallas kernels: 106 us -> 104 us  [local(): pl.pallas_call(_kernel, out_shape=shapes, in_specs=[vmem, vmem, vmem, hbm...]
where the time goes in v3:
time: 107 us
  Pallas kernels  106 us (99%)
    pallas_call x1, Pallas kernels, local(): pl.pallas_call(_kernel, out_shape=shapes, in_specs=[vmem, vmem, vmem, hbm...  104 us

profile of v3, /device:TPU:1, one launch (start us, length us, event | category | flops | bytes accessed | tf_op | source)
XLA Modules:
  0.0 106.8 jit_solution(8279000239144376551)
XLA Ops:
  0.6 104.4 %shard_map.85 = (bf16[128,256]{1,0:T(8,128)(2,1)}, f32[256,256]{1,0:T(8,128)}, bf16[128,256]{1,0:T(8,128)(2,1)}) custom-call(bf16[128,256]{1,0:T(8,128)(2,1)} %feat.1, bf16[256,256]{1,0:T(8,128)(2,1)} %weight.1, bf16[128,256]{1,0:T(8,128)(2,1)} %cot.1, bf16[12288,128]{1,0:T(8,128)(2,1)} %bitcast.7, s32[24,64]{1,0:T(8,128)} %bitcast.8, s32[24,64]{1,0:T(8,128)} %bitcast.9, ...), custom_call_target="tpu_custom_call" | custom-call | tf_op jit(solution)/shard_map/pallas_call | solution.py:366
  105.1 1.7 %shard_map.86 = (bf16[128,256]{1,0:T(8,128)(2,1)}, f32[256,256]{1,0:T(8,128)}, bf16[128,256]{1,0:T(8,128)(2,1)}) custom-call(bf16[128,256]{1,0:T(8,128)(2,1)} %get-tuple-element.6.a, f32[256,256]{1,0:T(8,128)} %get-tuple-element.7.b, bf16[128,256]{1,0:T(8,128)(2,1)} %get-tuple-element.8.c), custom_call_target="tpu_custom_call" | custom-call | tf_op jit(solution)/shard_map/pallas_call | solution.py:412

commit v4 on v3

--- a/solution.py
+++ b/solution.py
@@ -18,6 +18,8 @@
 NZ = ZH * ZL
 SLOT = 24
 MSG = ZH * SLOT
+OTHER = MSG - SLOT
+OWN = ZH - 1
 BLK = 128
 F = 256
 PER_COL = 8
@@ -39,9 +41,10 @@
 def _kernel(
     feat, weight, cot, tiles, src, srcs, dsts,
     out, gw, gx,
-    X, tb, tf, G, A, AT, bcol, brow, krow, keys, U, T, s1, r1, acc, s2, r2, BI, s3, R, ts, town, rs,
+    X, tb, tf, G, A, AT, bcol, brow, krow, nat, keys, U, Uo, T, s1, r1, ro, acc, s2, r2, BI, s3, so, R, ts, town, rs,
     W, WA, w1, WB, WC, WD, WE,
-    loc_sem, ag_s, ag_r, k_s, k_r, y1_s, y1_r, z1_s, z1_r, z2_s, z2_r, y2_s, y2_r,
+    loc_sem, ag_s, ag_r, k_s, k_r, y1_s, y1_r, o1_s, o1_r, z1_s, z1_r, z2_s, z2_r,
+    y2_s, y2_r, o2_s, o2_r,
     rs_s, rs_r, a_s, a_r, b_s, b_r, c_s, c_r, d_s, d_r, e_s, e_r,
 ):
     r = lax.axis_index("rows")
@@ -82,22 +85,33 @@
 
     def y1(h):
         return lambda o, own: _copy(
-            s1.at[h, o], r1.at[h, own, pl.ds(0, MSG)], y1_s.at[h, o], y1_r.at[h, own], *plane(o)
-        )
-
-    def z1(h):
-        return lambda o, own: _copy(
-            s2.at[h, o], r2.at[h, own], z1_s.at[h, o], z1_r.at[h, own], *column(o)
-        )
-
-    def z2(h):
-        return lambda o, own: _copy(
-            BI.at[h, zh], BI.at[h, own], z2_s.at[h, o], z2_r.at[h, own], *column(o)
-        )
+            s1.at[h, o, pl.ds(0, OTHER)], r1.at[h, own, pl.ds(0, OTHER)],
+            y1_s.at[h, o], y1_r.at[h, own], *plane(o),
+        )
+
+    def o1(o, own):
+        return _copy(
+            s1.at[:, o, pl.ds(OTHER, SLOT)], ro.at[:, own, pl.ds(OTHER, SLOT)],
+            o1_s.at[o], o1_r.at[own], *plane(o),
+        )
+
+    def place(q):
+        return lax.rem(zh + 1 + q, ZH)
+
+    def z1(h, q, at):
+        return _copy(s2.at[h, q], r2.at[h, at], z1_s.at[h, q], z1_r.at[h, at], *column(place(q)))
+
+    def z2(h, q, at):
+        return _copy(BI.at[h, OWN], BI.at[h, at], z2_s.at[h, q], z2_r.at[h, at], *column(place(q)))
 
     def y2(h):
         return lambda o, own: _copy(
-            s3.at[h, o], R.at[h, own, pl.ds(0, MSG)], y2_s.at[h, o], y2_r.at[h, own], *plane(o)
+            s3.at[h, o], R.at[h, own, pl.ds(0, OTHER)], y2_s.at[h, o], y2_r.at[h, own], *plane(o)
+        )
+
+    def o2(o, own):
+        return _copy(
+            so.at[:, o], R.at[:, own, pl.ds(OTHER, SLOT)], o2_s.at[o], o2_r.at[own], *plane(o)
         )
 
     def rx(h):
@@ -154,7 +168,9 @@
 
     def clear(jj, carry):
         for h in range(2):
-            r1[h, jj, MSG:BLK, :] = jnp.zeros((BLK - MSG, BLK), BF)
+            r1[h, jj, OTHER:BLK, :] = jnp.zeros((BLK - OTHER, BLK), BF)
+            ro[h, jj, 0:OTHER, :] = jnp.zeros((OTHER, BLK), BF)
+            ro[h, jj, MSG:BLK, :] = jnp.zeros((BLK - MSG, BLK), BF)
             R[h, jj, MSG:BLK, :] = jnp.zeros((BLK - MSG, BLK), BF)
         return carry
 
@@ -174,10 +190,13 @@
     padding = jnp.full((BLK - MSG, BLK), -1.0, F32)
     for jj in range(NJ):
         peers = [((jj // NC) * ZH + h) * NC + jj % NC for h in range(ZH)]
-        blocks = [jnp.broadcast_to(block[:, p : p + 1], (SLOT, BLK)) for p in peers]
-        heads = [jnp.broadcast_to(landing[:, p : p + 1], (SLOT, BLK)) for p in peers]
-        heads = [jnp.where(v < BLK, v + float(h * BLK), -1.0) for h, v in enumerate(heads)]
-        blocks = jnp.concatenate([*blocks, padding], axis=0)
+        for h, p in enumerate(peers):
+            nat[0, h * SLOT : (h + 1) * SLOT] = jnp.broadcast_to(block[:, p : p + 1], (SLOT, BLK))
+            nat[1, h * SLOT : (h + 1) * SLOT] = jnp.broadcast_to(landing[:, p : p + 1], (SLOT, BLK))
+        at = [pl.ds(pl.multiple_of(place(q) * SLOT, 8), SLOT) for q in range(ZH)]
+        heads = [nat[1, at[q]] for q in range(ZH)]
+        heads = [jnp.where(v < BLK, v + float(q * BLK), -1.0) for q, v in enumerate(heads)]
+        blocks = jnp.concatenate([*[nat[0, at[q]] for q in range(ZH)], padding], axis=0)
         bcol[jj] = blocks[0:MSG]
         brow[jj] = jnp.transpose(blocks)[0:1]
         krow[jj] = jnp.transpose(jnp.concatenate([*heads, padding], axis=0))[0:1]
@@ -186,10 +205,11 @@
 
     def gather(jj, carry):
         first = lax.div(jj, NC) * (ZH * NC) + lax.rem(jj, NC)
-        for h in range(ZH):
+        for q in range(ZH):
+            peer = first + place(q) * NC
             for i in range(SLOT):
-                at = h * SLOT + i
-                G[jj, at : at + 1, :] = tf[pl.ds(src[i, first + h * NC], 1), :]
+                at = q * SLOT + i
+                G[jj, at : at + 1, :] = tf[pl.ds(src[i, peer], 1), :]
         rows = G[jj, 0:MSG, :]
         where = bcol[jj]
         for b in range(NCOL):
@@ -198,13 +218,13 @@
 
     lax.fori_loop(0, NJ, gather, 0)
 
-    def fan_out(h, left, right, width, held, make):
+    def fan_out(left, right, width, hold, make):
         for t in range(NJ // 4):
             at = lax.rem(lax.div(j, 4) + t, 4) * 4
             rows = jnp.dot(
                 left[pl.ds(at, 4)].reshape(4 * MSG, width), right, preferred_element_type=F32
             )
-            held[h, pl.ds(at, 4)] = rows.reshape(4, MSG, BLK).astype(BF)
+            hold(pl.ds(at, 4), rows.reshape(4, MSG, BLK))
             for u in range(4):
                 o = at + lax.rem(j + u, 4)
 
@@ -214,8 +234,14 @@
 
     for h in range(2):
         arrive(ag(h), NREP, c)
-        fan_out(h, A, X[h].reshape(NREP * BLK, BLK), NREP * BLK, s1, y1(h))
-        r1[h, j, 0:MSG, :] = s1[h, j]
+
+        def hold(at, rows):
+            s1[h, at] = rows.astype(BF)
+
+        fan_out(A, X[h].reshape(NREP * BLK, BLK), NREP * BLK, hold, y1(h))
+        r1[h, j, 0:OTHER, :] = s1[h, j, 0:OTHER, :]
+        ro[h, j, OTHER:MSG, :] = s1[h, j, OTHER:MSG, :]
+    start(o1, NJ, j)
 
     arrive(kx, NJ, j)
     lanes = lax.broadcasted_iota(jnp.int32, (MSG, BLK), 1).astype(F32)
@@ -224,11 +250,14 @@
     def mirror(jj, carry):
         at = pl.multiple_of(jj * BLK, BLK)
         T[:, pl.ds(at, BLK)] = jnp.where(keys[jj] == heads, 1.0, 0.0).astype(BF)
-        where = jnp.transpose(jnp.broadcast_to(keys[jj], (BLK, BLK)))[0:MSG, :]
+        where = jnp.transpose(jnp.broadcast_to(keys[jj], (BLK, BLK)))
         for h in range(ZH):
             U[jj, :, h * BLK : (h + 1) * BLK] = jnp.where(
-                where == lanes + float(h * BLK), 1.0, 0.0
+                where[0:MSG] == lanes + float(h * BLK), 1.0, 0.0
             ).astype(BF)
+        Uo[jj] = jnp.where(
+            where[OTHER : OTHER + 32] == lanes[0:32] + float(OWN * BLK), 1.0, 0.0
+        ).astype(BF)
         turned = jnp.transpose(G[jj])
         row = brow[jj]
         for b in range(NCOL):
@@ -238,21 +267,30 @@
     lax.fori_loop(0, NJ, mirror, 0)
 
     for h in range(2):
+        sent(ag(h), NREP, c)
+    sent(kx, NJ, j)
+
+    for h in range(2):
         arrive(y1(h), NJ, j)
-        acc[h] = jnp.dot(
-            T[...], r1[h].reshape(NJ * BLK, BLK), preferred_element_type=F32
-        ).reshape(ZH, BLK, BLK)
-        for k in range(1, ZH):
-            o = lax.rem(zh + k, ZH)
-            s2[h, o] = acc[h, o].astype(BF)
-            z1(h)(o, zh).start()
-
+        sums = jnp.dot(
+            T[0 : OWN * BLK], r1[h].reshape(NJ * BLK, BLK), preferred_element_type=F32
+        )
+        for q in range(OWN):
+            s2[h, q] = sums[q * BLK : (q + 1) * BLK].astype(BF)
+            z1(h, q, OWN - 1 - q).start()
+
+    arrive(o1, NJ, j)
+    for h in range(2):
+        acc[h] = feat[:, h * BLK : (h + 1) * BLK].astype(F32) + jnp.dot(
+            T[OWN * BLK :], ro[h].reshape(NJ * BLK, BLK), preferred_element_type=F32
+        )
     halves = []
     for h in range(2):
-        total = feat[:, h * BLK : (h + 1) * BLK].astype(F32) + acc[h, zh]
-        arrive(z1(h), ZH, zh)
-        for k in range(1, ZH):
-            total += r2[h, lax.rem(zh + k, ZH)].astype(F32)
+        total = acc[h]
+        for q in range(OWN):
+            z1(h, q, q).wait_recv()
+        for q in range(OWN):
+            total += r2[h, q].astype(F32)
         halves.append(total.astype(BF))
     aggregated = jnp.concatenate(halves, axis=1)
 
@@ -263,8 +301,14 @@
         pre_grad, weight[...], (((1,), (1,)), ((), ())), preferred_element_type=F32
     ).astype(BF)
     for h in range(2):
-        BI[h, zh] = back_in[:, h * BLK : (h + 1) * BLK]
-        start(z2(h), ZH, zh)
+        BI[h, OWN] = back_in[:, h * BLK : (h + 1) * BLK]
+        for q in range(OWN):
+            z2(h, q, OWN - 1 - q).start()
+    for h in range(2):
+        rows = jnp.dot(Uo[...].reshape(NJ * 32, BLK), BI[h, OWN], preferred_element_type=F32)
+        so[h] = rows.reshape(NJ, 32, BLK)[:, 0:SLOT].astype(BF)
+        R[h, j, OTHER:MSG, :] = so[h, j]
+    start(o2, NJ, j)
 
     local_w = lax.dot_general(
         aggregated, pre_grad, (((0,), (0,)), ((), ())), preferred_element_type=F32
@@ -281,9 +325,14 @@
     start(gb, NY, y)
 
     for h in range(2):
-        arrive(z2(h), ZH, zh)
-        fan_out(h, U, BI[h].reshape(ZH * BLK, BLK), ZH * BLK, s3, y2(h))
-        R[h, j, 0:MSG, :] = s3[h, j]
+        for q in range(OWN):
+            z2(h, q, q).wait_recv()
+
+        def hold(at, rows):
+            s3[h, at] = rows[:, 0:OTHER].astype(BF)
+
+        fan_out(U, BI[h].reshape(ZH * BLK, BLK), ZH * BLK, hold, y2(h))
+        R[h, j, 0:OTHER, :] = s3[h, j]
 
     arrive(gb, NY, y)
     total = w1[y]
@@ -298,6 +347,17 @@
     WD[y] = total * (1.0 / math.sqrt(NODES))
     start(gd, NY, y)
 
+    for h in range(2):
+        sent(y1(h), NJ, j)
+        for q in range(OWN):
+            z1(h, q, q).wait_send()
+            z2(h, q, q).wait_send()
+    sent(o1, NJ, j)
+    sent(ga, NM, m)
+    sent(gb, NY, y)
+    sent(gc, NZ, z)
+
+    arrive(o2, NJ, j)
     for h in range(2):
         arrive(y2(h), NJ, j)
         for t in range(ZL):
@@ -321,9 +381,14 @@
             arrive(gd, NY, y)
             WE[m] = WD[...]
             start(ge, NM, m)
-
-    for h in range(2):
-        result = BI[h, zh].astype(F32) + town[h, x]
+            sent(o2, NJ, j)
+            sent(y2(0), NJ, j)
+
+    sent(y2(1), NJ, j)
+    sent(rx(0), NREP, c)
+    sent(gd, NY, y)
+    for h in range(2):
+        result = BI[h, OWN].astype(F32) + town[h, x]
         arrive(rx(h), NREP, c)
         for k in range(1, NREP):
             result += rs[h, lax.rem(c + k, NREP)].astype(F32)
@@ -333,15 +398,8 @@
     for h in range(2):
         gw[:, h * BLK : (h + 1) * BLK] = WE[h * NM // 2 : (h + 1) * NM // 2].reshape(F, BLK)
 
-    for make, count, me in (
-        (ag, NREP, c), (y1, NJ, j), (z1, ZH, zh), (z2, ZH, zh), (y2, NJ, j), (rx, NREP, c),
-    ):
-        for h in range(2):
-            sent(make(h), count, me)
-    for make, count, me in (
-        (kx, NJ, j), (ga, NM, m), (gb, NY, y), (gc, NZ, z), (gd, NY, y), (ge, NM, m),
-    ):
-        sent(make, count, me)
+    sent(ge, NM, m)
+    sent(rx(1), NREP, c)
 
 
 def _leave(a, b, c, aa, bb, cc):
@@ -378,16 +436,20 @@
             V((NJ, MSG, BLK), F32),
             V((NJ, 1, BLK), F32),
             V((NJ, 1, BLK), F32),
+            V((2, MSG, BLK), F32),
             V((NJ, 1, BLK), F32),
             V((NJ, MSG, ZH * BLK), BF),
+            V((NJ, 32, BLK), BF),
             V((ZH * BLK, NJ * BLK), BF),
             V((2, NJ, MSG, BLK), BF),
             V((2, NJ, BLK, BLK), BF),
-            V((2, ZH, BLK, BLK), F32),
+            V((2, NJ, BLK, BLK), BF),
+            V((2, BLK, BLK), F32),
+            V((2, OWN, BLK, BLK), BF),
+            V((2, OWN, BLK, BLK), BF),
             V((2, ZH, BLK, BLK), BF),
-            V((2, ZH, BLK, BLK), BF),
-            V((2, ZH, BLK, BLK), BF),
-            V((2, NJ, MSG, BLK), BF),
+            V((2, NJ, OTHER, BLK), BF),
+            V((2, NJ, SLOT, BLK), BF),
             V((2, NJ, BLK, BLK), BF),
             V((2, NREP, BLK, BLK), BF),
             V((2, NX, BLK, BLK), F32),
@@ -400,9 +462,13 @@
             V((NY, 8, BLK), F32),
             V((NM, NY, 8, BLK), F32),
             dma,
-            dma((2, NREP)), dma((2, NREP)), dma((NJ,)), dma((NJ,)), dma((2, NJ)), dma((2, NJ)),
-            dma((2, ZH)), dma((2, ZH)), dma((2, ZH)), dma((2, ZH)), dma((2, NJ)), dma((2, NJ)),
-            dma((2, NREP)), dma((2, NREP)),
+            *[
+                dma(n)
+                for n in (
+                    (2, NREP), (NJ,), (2, NJ), (NJ,), (2, OWN), (2, OWN), (2, NJ), (NJ,), (2, NREP),
+                )
+                for _ in range(2)
+            ],
             *[dma((n,)) for n in (NM, NY, NZ, NY, NM) for _ in range(2)],
         ],
         compiler_params=pltpu.CompilerParams(

time: 107 us -> 101 us (0.944)
  Pallas kernels: 106 us -> 99.6 us
    pallas_call x1, Pallas kernels: 104 us -> 97.9 us  [local(): pl.pallas_call(_kernel, out_shape=shapes, in_specs=[vmem, vmem, vmem, hbm...]
where the time goes in v4:
time: 101 us; the launch traced here: 100 us
  Pallas kernels  99.6 us (99%)
    pallas_call x1, Pallas kernels, local(): pl.pallas_call(_kernel, out_shape=shapes, in_specs=[vmem, vmem, vmem, hbm...  97.9 us

profile of v4, /device:TPU:1, one launch (start us, length us, event | category | flops | bytes accessed | tf_op | source)
XLA Modules:
  0.0 100.2 jit_solution(5706166032121469700)
XLA Ops:
  0.6 97.9 %shard_map.85 = (bf16[128,256]{1,0:T(8,128)(2,1)}, f32[256,256]{1,0:T(8,128)}, bf16[128,256]{1,0:T(8,128)(2,1)}) custom-call(bf16[128,256]{1,0:T(8,128)(2,1)} %feat.1, bf16[256,256]{1,0:T(8,128)(2,1)} %weight.1, bf16[128,256]{1,0:T(8,128)(2,1)} %cot.1, bf16[12288,128]{1,0:T(8,128)(2,1)} %bitcast.7, s32[24,64]{1,0:T(8,128)} %bitcast.8, s32[24,64]{1,0:T(8,128)} %bitcast.9, ...), custom_call_target="tpu_custom_call" | custom-call | tf_op jit(solution)/shard_map/pallas_call | solution.py:424
  98.5 1.7 %shard_map.86 = (bf16[128,256]{1,0:T(8,128)(2,1)}, f32[256,256]{1,0:T(8,128)}, bf16[128,256]{1,0:T(8,128)(2,1)}) custom-call(bf16[128,256]{1,0:T(8,128)(2,1)} %get-tuple-element.6.a, f32[256,256]{1,0:T(8,128)} %get-tuple-element.7.b, bf16[128,256]{1,0:T(8,128)(2,1)} %get-tuple-element.8.c), custom_call_target="tpu_custom_call" | custom-call | tf_op jit(solution)/shard_map/pallas_call | solution.py:478
